TPU v7x, 32 devices: a whole 2x2x4 slice. The times are simulated.
32 devices in a mesh: ctx: 8 (over y, x, core), fsdp: 4 (over z).
Axes of the slice: x: 2, y: 2, z: 4, core: 2. Of those that a mesh axis runs over, the one named last changes fastest.
Arguments:
- tokens: bfloat16 [10240, 768], P(('ctx', 'fsdp')), may hold values from -6 to 6
- lengths: int32 [4, 3], P('fsdp'), may hold values from 1 to 1280, 2560 in all within a row
- deal_table: int32 [4, 8, 8], P('fsdp'), may hold values from 0 to 7, each once within a row
- norm_one_gain: bfloat16 [768], P('fsdp'), may hold values from 0.099609375 to 1.8984375
- norm_one_bias: bfloat16 [768], P('fsdp'), may hold values from -3 to 3
- triple_weight: bfloat16 [768, 2304], P('fsdp'), may hold values from -1 to 1
- output_weight: bfloat16 [768, 768], P('fsdp'), may hold values from -0.4375 to 0.4375
- norm_two_gain: bfloat16 [768], P('fsdp'), may hold values from 0.099609375 to 1.8984375
- norm_two_bias: bfloat16 [768], P('fsdp'), may hold values from -3 to 3
- up_weight: bfloat16 [768, 3072], P('fsdp'), may hold values from -0.21875 to 0.21875
- down_weight: bfloat16 [3072, 768], P('fsdp'), may hold values from -0.15625 to 0.15625
- cotangent: bfloat16 [10240, 768], P(('ctx', 'fsdp')), may hold values from -6 to 6
Outputs:
- result: bfloat16 [10240, 768], P(('ctx', 'fsdp'))
- token_grad: float32 [10240, 768], P(('ctx', 'fsdp'))
- norm_one_gain_grad: float32 [768], P('fsdp')
- norm_one_bias_grad: float32 [768], P('fsdp')
- triple_weight_grad: float32 [768, 2304], P('fsdp')
- output_weight_grad: float32 [768, 768], P('fsdp')
- norm_two_gain_grad: float32 [768], P('fsdp')
- norm_two_bias_grad: float32 [768], P('fsdp')
- up_weight_grad: float32 [768, 3072], P('fsdp')
- down_weight_grad: float32 [3072, 768], P('fsdp')
Inputs may be any that keep to these rules, and one draw needn't show every extreme that they name: Row f gives the lengths of the 3 sequences packed in order into group f's 2560 positions; they sum to 2560, and the longest is exactly 1280. For every group f and natural block s, deal_table[f, s] is a permutation of 0 .. 7.
All inputs are finite; a program needn't handle non-finite values.
Results may differ from a plain program's by a relative error of at most 0.025.
The roundings to bfloat16 on the way count: a program that leaves them out, or rounds other values in their place, can miss the bound.
Values may be sent and summed in bfloat16 or wider, within the bound.
No kernel may reach another device: no remote copies, remote signals or barrier semaphores. Data moves between devices by JAX's collectives and lax.ppermute only.
A program may use at most 256 MiB of HBM per device.

v0:
```python
import math

import jax
import jax.numpy as jnp
from jax import lax
from jax.sharding import PartitionSpec as P

HEADS = 12
HEAD = 64


EPS = 1e-05


def entering(part, axis, combine, identity, reverse):
    count = lax.axis_size(axis)
    place = lax.axis_index(axis)
    ahead = count - 1 - place if reverse else place
    gathered = lax.all_gather(part, axis)
    state = jnp.zeros_like(part) + jnp.asarray(identity, part.dtype)

    def one(turn, state):
        source = count - 1 - turn if reverse else turn
        return combine(state, lax.dynamic_index_in_dim(gathered, source, 0, False))

    return lax.fori_loop(0, ahead, one, state)


def layer_norm(values, gain_vec, offset):
    center = values - jnp.mean(values, axis=-1, keepdims=True)
    spread = jnp.mean(center * center, axis=-1, keepdims=True)
    return center * lax.rsqrt(spread + EPS) * gain_vec + offset


def norm_back(values, gain_vec, offset, grad_vec):
    unused, pullback = jax.vjp(layer_norm, values, gain_vec, offset)
    return pullback(grad_vec)


def gelu_back(values, grad_vec):
    unused, pullback = jax.vjp(jax.nn.gelu, values)
    return pullback(grad_vec)[0]


def matmul(left_side, right_side):
    return jnp.dot(left_side, right_side, preferred_element_type=jnp.float32)


def cross_rows(left_side, right_side):
    return lax.dot_general(
        left_side, right_side, (((0,), (0,)), ((), ())), preferred_element_type=jnp.float32
    )


def cross_cols(left_side, right_side):
    return lax.dot_general(
        left_side, right_side, (((1,), (1,)), ((), ())), preferred_element_type=jnp.float32
    )


def add_pair(earlier, latest):
    return earlier + latest


def body(
    tokens,
    lengths,
    deal_table,
    norm_one_gain,
    norm_one_bias,
    triple_weight,
    output_weight,
    norm_two_gain,
    norm_two_bias,
    up_weight,
    down_weight,
    cotangent,
):
    n_ctx = lax.axis_size("ctx")
    device = lax.axis_index("ctx")
    row_count, model_width = tokens.shape
    part_rows = row_count // n_ctx
    group_rows = row_count * n_ctx
    key_rows = 2 * row_count
    blocks = group_rows // key_rows
    head_scale = 1.0 / math.sqrt(HEAD)
    route_table = deal_table[0]
    counter = jnp.arange(n_ctx, dtype=jnp.int32)
    route_hits = route_table[:, :, None] == counter[None, None, :]
    inverse = jnp.sum(jnp.where(route_hits, counter[None, :, None], 0), axis=1)
    my_parts = jnp.take(inverse, device, axis=0)
    my_owners = jnp.take(route_table, device, axis=0)
    offsets = counter[:, None] * row_count + inverse * part_rows
    within = jnp.arange(part_rows, dtype=jnp.int32)
    key_pos = (offsets.T[:, :, None] + within[None, None, :]).reshape(group_rows)
    query_pos = (jnp.take(offsets, device, axis=1)[:, None] + within[None, :]).reshape(row_count)
    seq_lens = lengths[0]
    seq_ends = jnp.cumsum(seq_lens)
    seq_starts = seq_ends - seq_lens
    key_seg = jnp.sum((key_pos[:, None] >= seq_ends[None, :]).astype(jnp.int32), axis=1)
    key_first = jnp.any(key_pos[:, None] == seq_starts[None, :], axis=1)
    query_seg = jnp.sum((query_pos[:, None] >= seq_ends[None, :]).astype(jnp.int32), axis=1)
    gain_one, bias_one, triple_full, output_full, gain_two, bias_two, up_full, down_full = (
        lax.all_gather(norm_one_gain, "fsdp", axis=0, tiled=True),
        lax.all_gather(norm_one_bias, "fsdp", axis=0, tiled=True),
        lax.all_gather(triple_weight, "fsdp", axis=0, tiled=True),
        lax.all_gather(output_weight, "fsdp", axis=0, tiled=True),
        lax.all_gather(norm_two_gain, "fsdp", axis=0, tiled=True),
        lax.all_gather(norm_two_bias, "fsdp", axis=0, tiled=True),
        lax.all_gather(up_weight, "fsdp", axis=0, tiled=True),
        lax.all_gather(down_weight, "fsdp", axis=0, tiled=True),
    )
    gain_one = gain_one.astype(jnp.float32)
    bias_one = bias_one.astype(jnp.float32)
    gain_two = gain_two.astype(jnp.float32)
    bias_two = bias_two.astype(jnp.float32)
    outgoing = jnp.take(tokens.reshape(n_ctx, part_rows, model_width), my_parts, axis=0)
    dealt = lax.all_to_all(outgoing, "ctx", split_axis=0, concat_axis=0, tiled=True).reshape(
        row_count, model_width
    )
    resid = dealt.astype(jnp.float32)
    hidden_one = layer_norm(resid, gain_one, bias_one).astype(jnp.bfloat16)
    projected = matmul(hidden_one, triple_full).astype(jnp.bfloat16)
    queries = projected[:, :model_width]
    key_part = projected[:, model_width : 2 * model_width]
    value_part = projected[:, 2 * model_width :]
    all_keys, all_values = (
        lax.all_gather(key_part, "ctx", axis=0, tiled=True),
        lax.all_gather(value_part, "ctx", axis=0, tiled=True),
    )
    query_heads = queries.reshape(row_count, HEADS, HEAD)
    query_first = query_heads[:, 0, :]
    key_blocks = all_keys.reshape(blocks, key_rows, HEADS, HEAD)
    value_blocks = all_values.reshape(blocks, key_rows, HEADS, HEAD)
    pos_blocks = key_pos.reshape(blocks, key_rows)
    seg_blocks = key_seg.reshape(blocks, key_rows)
    first_blocks = key_first.reshape(blocks, key_rows)

    def make_masks(pos_key, seg_key, first_key):
        same_seq = query_seg[:, None] == seg_key[None, :]
        allowed = same_seq & (pos_key[None, :] <= query_pos[:, None])
        chosen = (
            same_seq & (pos_key[None, :] < query_pos[:, None]) & jnp.logical_not(first_key)[None, :]
        )
        return (allowed, chosen)

    def first_logits(key_block):
        return cross_cols(query_first, key_block[:, 0, :]) * head_scale

    def select_of(logit_first, chosen):
        return jnp.where(chosen, jax.nn.relu(logit_first), 0.0)

    def prior_of(select, carried):
        shaped = select.reshape(n_ctx, part_rows, key_rows)
        return (carried[:, None, :] + jnp.cumsum(shaped, axis=1) - shaped).reshape(
            row_count, key_rows
        )

    def exponent(key_block, pos_key, seg_key, first_key, carried):
        logits = (
            jnp.einsum("qhe,khe->hqk", query_heads, key_block, preferred_element_type=jnp.float32)
            * head_scale
        )
        allowed, chosen = make_masks(pos_key, seg_key, first_key)
        prior_sum = prior_of(select_of(logits[0], chosen), carried)
        return jnp.where(allowed[None], jnp.exp(logits - prior_sum[None]), 0.0)

    def pass_sums(carry_state, scan_inputs):
        key_block, pos_key, seg_key, first_key = scan_inputs
        allowed, chosen = make_masks(pos_key, seg_key, first_key)
        select = select_of(first_logits(key_block), chosen)
        return (carry_state, jnp.sum(select.reshape(n_ctx, part_rows, key_rows), axis=1))

    unused, block_sums = lax.scan(
        pass_sums, jnp.zeros((), jnp.float32), (key_blocks, pos_blocks, seg_blocks, first_blocks)
    )
    part_sums = block_sums.transpose(1, 0, 2).reshape(n_ctx, group_rows)
    arrived = lax.all_to_all(part_sums, "ctx", split_axis=0, concat_axis=0, tiled=True)
    ordered = jnp.take(arrived, my_owners, axis=0)
    block_total = jnp.sum(ordered, axis=0)
    before = entering(block_total, "ctx", add_pair, jnp.zeros_like(block_total), False)
    prefix = before[None, :] + jnp.cumsum(ordered, axis=0) - ordered
    carried_all = lax.all_to_all(
        jnp.take(prefix, my_parts, axis=0), "ctx", split_axis=0, concat_axis=0, tiled=True
    )
    carried_blocks = carried_all.reshape(n_ctx, blocks, key_rows).transpose(1, 0, 2)

    def pass_attend(carry_state, scan_inputs):
        key_block, value_block, pos_key, seg_key, first_key, carried = scan_inputs
        numer_sum, total_sum = carry_state
        expo_block = exponent(key_block, pos_key, seg_key, first_key, carried)
        numer_sum = numer_sum + jnp.einsum(
            "hqk,khe->qhe",
            expo_block.astype(jnp.bfloat16),
            value_block,
            preferred_element_type=jnp.float32,
        )
        total_sum = total_sum + jnp.sum(expo_block, axis=-1)
        return ((numer_sum, total_sum), None)

    start_state = (
        jnp.zeros((row_count, HEADS, HEAD), jnp.float32),
        jnp.zeros((HEADS, row_count), jnp.float32),
    )
    main_inputs = (key_blocks, value_blocks, pos_blocks, seg_blocks, first_blocks, carried_blocks)
    (numer_sum, total_sum), unused = lax.scan(pass_attend, start_state, main_inputs)
    attn_mixed = numer_sum / total_sum.T[:, :, None]
    mixed_low = attn_mixed.reshape(row_count, model_width).astype(jnp.bfloat16)
    middle = resid + matmul(mixed_low, output_full)
    hidden_two = layer_norm(middle, gain_two, bias_two).astype(jnp.bfloat16)
    raised = matmul(hidden_two, up_full)
    activated = jax.nn.gelu(raised).astype(jnp.bfloat16)
    result = (middle + matmul(activated, down_full)).astype(jnp.bfloat16)
    grad_final = cotangent.astype(jnp.float32)
    grad_down = cross_rows(activated, cotangent)
    grad_raised = gelu_back(raised, cross_cols(cotangent, down_full)).astype(jnp.bfloat16)
    grad_up = cross_rows(hidden_two, grad_raised)
    grad_hidden_two = cross_cols(grad_raised, up_full)
    grad_mid_norm, grad_gain_two, grad_bias_two = norm_back(
        middle, gain_two, bias_two, grad_hidden_two
    )
    grad_middle = grad_final + grad_mid_norm
    grad_attended = grad_middle.astype(jnp.bfloat16)
    grad_output = cross_rows(mixed_low, grad_attended)
    grad_mixed = cross_cols(grad_attended, output_full).reshape(row_count, HEADS, HEAD)
    scaled_low = (grad_mixed / total_sum.T[:, :, None]).astype(jnp.bfloat16)
    row_ratio = jnp.sum(grad_mixed * attn_mixed, axis=-1).T / total_sum

    def phase_main(carry_state, scan_inputs):
        key_block, value_block, pos_key, seg_key, first_key, carried = scan_inputs
        expo_block = exponent(key_block, pos_key, seg_key, first_key, carried)
        back_expo = jnp.einsum(
            "qhe,khe->hqk", scaled_low, value_block, preferred_element_type=jnp.float32
        )
        grad_logit = expo_block * (back_expo - row_ratio[:, :, None])
        grad_prior = -jnp.sum(grad_logit, axis=0)
        rest_low = grad_logit[1:].astype(jnp.bfloat16)
        carry_state = (
            carry_state
            + jnp.einsum(
                "hqk,khe->qhe", rest_low, key_block[:, 1:], preferred_element_type=jnp.float32
            )
            * head_scale
        )
        part_grad = jnp.sum(grad_prior.reshape(n_ctx, part_rows, key_rows), axis=1)
        grad_value = jnp.einsum(
            "hqk,qhe->khe",
            expo_block.astype(jnp.bfloat16),
            scaled_low,
            preferred_element_type=jnp.float32,
        )
        grad_key_rest = (
            jnp.einsum(
                "hqk,qhe->khe", rest_low, query_heads[:, 1:], preferred_element_type=jnp.float32
            )
            * head_scale
        )
        return (carry_state, (grad_prior, part_grad, grad_value, grad_key_rest))

    query_rest, main_out = lax.scan(
        phase_main, jnp.zeros((row_count, HEADS - 1, HEAD), jnp.float32), main_inputs
    )
    grad_priors = main_out[0]
    part_grads = main_out[1]
    value_grad = main_out[2].reshape(group_rows, model_width)
    key_rest_grad = main_out[3].reshape(group_rows, model_width - HEAD)
    arrived_grad = lax.all_to_all(
        part_grads.transpose(1, 0, 2).reshape(n_ctx, group_rows),
        "ctx",
        split_axis=0,
        concat_axis=0,
        tiled=True,
    )
    ordered_grad = jnp.take(arrived_grad, my_owners, axis=0)
    grad_total = jnp.sum(ordered_grad, axis=0)
    after_sum = entering(grad_total, "ctx", add_pair, jnp.zeros_like(grad_total), True)
    suffix = (
        after_sum[None, :]
        + jnp.flip(jnp.cumsum(jnp.flip(ordered_grad, 0), axis=0), 0)
        - ordered_grad
    )
    later_all = lax.all_to_all(
        jnp.take(suffix, my_parts, axis=0), "ctx", split_axis=0, concat_axis=0, tiled=True
    )
    later_blocks = later_all.reshape(n_ctx, blocks, key_rows).transpose(1, 0, 2)

    def phase_first(carry_state, scan_inputs):
        key_block, value_block, pos_key, seg_key, first_key, carried, later_cols, grad_prior = (
            scan_inputs
        )
        allowed, chosen = make_masks(pos_key, seg_key, first_key)
        logit_first = first_logits(key_block)
        prior_sum = prior_of(select_of(logit_first, chosen), carried)
        expo_first = jnp.where(allowed, jnp.exp(logit_first - prior_sum), 0.0)
        back_first = cross_cols(scaled_low[:, 0, :], value_block[:, 0, :])
        grad_first = expo_first * (back_first - row_ratio[0][:, None])
        shaped = grad_prior.reshape(n_ctx, part_rows, key_rows)
        tail_sum = (
            later_cols[:, None, :] + jnp.flip(jnp.cumsum(jnp.flip(shaped, 1), axis=1), 1) - shaped
        ).reshape(row_count, key_rows)
        grad_first = grad_first + jnp.where(chosen & (logit_first > 0), tail_sum, 0.0)
        first_low = grad_first.astype(jnp.bfloat16)
        carry_state = carry_state + matmul(first_low, key_block[:, 0, :]) * head_scale
        return (carry_state, cross_rows(first_low, query_first) * head_scale)

    first_inputs = (
        key_blocks,
        value_blocks,
        pos_blocks,
        seg_blocks,
        first_blocks,
        carried_blocks,
        later_blocks,
        grad_priors,
    )
    query_first_grad, key_first_grads = lax.scan(
        phase_first, jnp.zeros((row_count, HEAD), jnp.float32), first_inputs
    )
    key_first_grad = key_first_grads.reshape(group_rows, HEAD)
    key_first_sum, key_rest_sum, value_sum = (
        lax.psum_scatter(key_first_grad, "ctx", scatter_dimension=0, tiled=True),
        lax.psum_scatter(key_rest_grad, "ctx", scatter_dimension=0, tiled=True),
        lax.psum_scatter(value_grad, "ctx", scatter_dimension=0, tiled=True),
    )
    query_grad = jnp.concatenate([query_first_grad[:, None, :], query_rest], axis=1).reshape(
        row_count, model_width
    )
    grad_projected = jnp.concatenate(
        [query_grad, key_first_sum, key_rest_sum, value_sum], axis=1
    ).astype(jnp.bfloat16)
    grad_triple = cross_rows(hidden_one, grad_projected)
    grad_hidden_one = cross_cols(grad_projected, triple_full)
    grad_res_norm, grad_gain_one, grad_bias_one = norm_back(
        resid, gain_one, bias_one, grad_hidden_one
    )
    grad_dealt = grad_middle + grad_res_norm
    returned = lax.all_to_all(
        grad_dealt.reshape(n_ctx, part_rows, model_width),
        "ctx",
        split_axis=0,
        concat_axis=0,
        tiled=True,
    )
    token_grad = jnp.take(returned, my_owners, axis=0).reshape(row_count, model_width)
    shard_g1, shard_b1, shard_triple, shard_output, shard_g2, shard_b2, shard_up, shard_down = (
        lax.psum_scatter(grad_gain_one, "fsdp", scatter_dimension=0, tiled=True),
        lax.psum_scatter(grad_bias_one, "fsdp", scatter_dimension=0, tiled=True),
        lax.psum_scatter(grad_triple, "fsdp", scatter_dimension=0, tiled=True),
        lax.psum_scatter(grad_output, "fsdp", scatter_dimension=0, tiled=True),
        lax.psum_scatter(grad_gain_two, "fsdp", scatter_dimension=0, tiled=True),
        lax.psum_scatter(grad_bias_two, "fsdp", scatter_dimension=0, tiled=True),
        lax.psum_scatter(grad_up, "fsdp", scatter_dimension=0, tiled=True),
        lax.psum_scatter(grad_down, "fsdp", scatter_dimension=0, tiled=True),
    )
    sum_g1, sum_b1, sum_triple, sum_output, sum_g2, sum_b2, sum_up, sum_down = lax.psum(
        (shard_g1, shard_b1, shard_triple, shard_output, shard_g2, shard_b2, shard_up, shard_down),
        "ctx",
    )
    return (
        result,
        token_grad,
        sum_g1,
        sum_b1,
        sum_triple,
        sum_output,
        sum_g2,
        sum_b2,
        sum_up,
        sum_down,
    )


def solution(mesh):
    return jax.shard_map(
        body,
        mesh=mesh,
        in_specs=(
            P(("ctx", "fsdp"), None),
            P("fsdp", None),
            P("fsdp", None, None),
            P("fsdp"),
            P("fsdp"),
            P("fsdp", None),
            P("fsdp", None),
            P("fsdp"),
            P("fsdp"),
            P("fsdp", None),
            P("fsdp", None),
            P(("ctx", "fsdp"), None),
        ),
        out_specs=(
            P(("ctx", "fsdp"), None),
            P(("ctx", "fsdp"), None),
            P("fsdp"),
            P("fsdp"),
            P("fsdp", None),
            P("fsdp", None),
            P("fsdp"),
            P("fsdp"),
            P("fsdp", None),
            P("fsdp", None),
        ),
        check_vma=False,
    )
```

profile of v0, /device:TPU:0, one launch (start us, length us, event | category | flops | bytes accessed | tf_op | source)
XLA Modules:
  0.0 1693.5 jit_solution(8925132901421102751)
XLA Ops:
  33.1 49.8 %all-gather.11.cloned.1.call-done = bf16[768,2304]{1,0:T(8,128)(2,1)} async-done(((bf16[192,2304]{1,0:T(8,128)(2,1)}), bf16[768,2304]{1,0:T(8,128)(2,1)}) %all-gather.11.cloned.1.call-update) | async-done | bytes 3538960 | tf_op jit(solution)/shard_map/all_gather | solution.py:106
  92.5 29.1 %all-gather.15.cloned.1.call-done = bf16[2560,768]{1,0:T(8,128)(2,1)} async-done(((bf16[320,768]{1,0:T(8,128)(2,1)}), bf16[2560,768]{1,0:T(8,128)(2,1)}) %all-gather.15.cloned.1.call-update) | async-done | bytes 3932176 | tf_op jit(solution)/shard_map/all_gather | solution.py:128
  171.5 41.0 %all-gather.21.cloned.1.call-done = bf16[3072,768]{1,0:T(8,128)(2,1)} async-done(((bf16[768,768]{1,0:T(8,128)(2,1)}), bf16[3072,768]{1,0:T(8,128)(2,1)}) %all-gather.21.cloned.1.call-update) | async-done | bytes 4718608 | tf_op jit(solution)/shard_map/all_gather | solution.py:111
  218.5 30.5 %all-gather.13.cloned.1.call-done = bf16[2560,768]{1,0:T(8,128)(2,1)} async-done(((bf16[320,768]{1,0:T(8,128)(2,1)}), bf16[2560,768]{1,0:T(8,128)(2,1)}) %all-gather.13.cloned.1.call-update) | async-done | bytes 3932176 | tf_op jit(solution)/shard_map/all_gather | solution.py:129
  268.0 40.6 %while.83 = (s32[]{:T(128)}, f32[320,12,64]{0,2,1:T(8,128)S(1)}, f32[12,320]{1,0:T(8,128)S(1)}, bf16[4,640,12,64]{1,3,2,0:T(8,128)(2,1)}, s32[320]{0:T(512)S(1)}...) while((s32[]{:T(128)}, f32[320,12,64]{0,2,1:T(8,128)S(1)}, ...), condition=%wide.region_17.20_spmd.clone, body=%wide.region_14.19_spmd.clone.sunk | while | flops 658313920 | bytes 43710920 | solution.py:206
  312.2 58.7 %all-gather.19.cloned.1.call-done = bf16[768,3072]{1,0:T(8,128)(2,1)} async-done(((bf16[192,3072]{1,0:T(8,128)(2,1)}), bf16[768,3072]{1,0:T(8,128)(2,1)}) %all-gather.19.cloned.1.call-update) | async-done | bytes 4718608 | tf_op jit(solution)/shard_map/all_gather | solution.py:110
  386.4 419.6 %while.84 = (s32[]{:T(128)}, f32[320,11,64]{0,2,1:T(8,128)}, f32[4,320,640]{2,1,0:T(8,128)}, f32[4,8,640]{2,1,0:T(8,128)S(1)}, f32[4,640,12,64]{1,0,3,2:T(4,128)...) while((s32[]{:T(128)}, f32[320,11,64]{0,2,1:T(8,128)}, ...), condition=%wide.region_27.30_spmd.clone, body=%wide.region_23.29_spmd.clone.sunk | while | flops 1557812224 | bytes 85669416 | solution.py:260
  418.4 35.0 %dynamic_update_slice.43 = f32[4,640,11,64]{1,0,3,2:T(4,128)} dynamic-update-slice(f32[4,640,11,64]{1,0,3,2:T(4,128)} %get-tuple-element.1554, f32[1,640,11,64]{1,0,3,2:T(1,128)} %copy.258, s32[]{:T(128)S(6)} %copy.301, s32[]{:T(128)} %constant.225.clone.1..sunk.3, s32[]{:T(128)} %constant.225.clone.1..sunk.3, s32[]{:T(128)} %constant.225.clone.1..sunk.3) | dynamic-update-slice | bytes 3604484 | tf_op jit(solution)/shard_map/while/body/jit(dynamic_update_index_in_dim)/dynamic_update_slice | solution.py:260
  453.4 37.8 %dynamic_update_slice.42 = f32[4,640,12,64]{1,0,3,2:T(4,128)} dynamic-update-slice(f32[4,640,12,64]{1,0,3,2:T(4,128)} %get-tuple-element.1553, f32[1,640,12,64]{1,0,3,2:T(1,128)S(1)} %copy.257, s32[]{:T(128)S(6)} %copy.301, s32[]{:T(128)} %constant.225.clone.1..sunk.3, s32[]{:T(128)} %constant.225.clone.1..sunk.3, s32[]{:T(128)} %constant.225.clone.1..sunk.3) | dynamic-update-slice | bytes 3932164 | tf_op jit(solution)/shard_map/while/body/jit(dynamic_update_index_in_dim)/dynamic_update_slice | solution.py:260
  523.3 35.0 %dynamic_update_slice.43 = f32[4,640,11,64]{1,0,3,2:T(4,128)} dynamic-update-slice(f32[4,640,11,64]{1,0,3,2:T(4,128)} %get-tuple-element.1554, f32[1,640,11,64]{1,0,3,2:T(1,128)} %copy.258, s32[]{:T(128)S(6)} %copy.301, s32[]{:T(128)} %constant.225.clone.1..sunk.3, s32[]{:T(128)} %constant.225.clone.1..sunk.3, s32[]{:T(128)} %constant.225.clone.1..sunk.3) | dynamic-update-slice | bytes 3604484 | tf_op jit(solution)/shard_map/while/body/jit(dynamic_update_index_in_dim)/dynamic_update_slice | solution.py:260
  558.3 37.8 %dynamic_update_slice.42 = f32[4,640,12,64]{1,0,3,2:T(4,128)} dynamic-update-slice(f32[4,640,12,64]{1,0,3,2:T(4,128)} %get-tuple-element.1553, f32[1,640,12,64]{1,0,3,2:T(1,128)S(1)} %copy.257, s32[]{:T(128)S(6)} %copy.301, s32[]{:T(128)} %constant.225.clone.1..sunk.3, s32[]{:T(128)} %constant.225.clone.1..sunk.3, s32[]{:T(128)} %constant.225.clone.1..sunk.3) | dynamic-update-slice | bytes 3932164 | tf_op jit(solution)/shard_map/while/body/jit(dynamic_update_index_in_dim)/dynamic_update_slice | solution.py:260
  628.2 35.0 %dynamic_update_slice.43 = f32[4,640,11,64]{1,0,3,2:T(4,128)} dynamic-update-slice(f32[4,640,11,64]{1,0,3,2:T(4,128)} %get-tuple-element.1554, f32[1,640,11,64]{1,0,3,2:T(1,128)} %copy.258, s32[]{:T(128)S(6)} %copy.301, s32[]{:T(128)} %constant.225.clone.1..sunk.3, s32[]{:T(128)} %constant.225.clone.1..sunk.3, s32[]{:T(128)} %constant.225.clone.1..sunk.3) | dynamic-update-slice | bytes 3604484 | tf_op jit(solution)/shard_map/while/body/jit(dynamic_update_index_in_dim)/dynamic_update_slice | solution.py:260
  663.2 37.8 %dynamic_update_slice.42 = f32[4,640,12,64]{1,0,3,2:T(4,128)} dynamic-update-slice(f32[4,640,12,64]{1,0,3,2:T(4,128)} %get-tuple-element.1553, f32[1,640,12,64]{1,0,3,2:T(1,128)S(1)} %copy.257, s32[]{:T(128)S(6)} %copy.301, s32[]{:T(128)} %constant.225.clone.1..sunk.3, s32[]{:T(128)} %constant.225.clone.1..sunk.3, s32[]{:T(128)} %constant.225.clone.1..sunk.3) | dynamic-update-slice | bytes 3932164 | tf_op jit(solution)/shard_map/while/body/jit(dynamic_update_index_in_dim)/dynamic_update_slice | solution.py:260
  733.1 35.0 %dynamic_update_slice.43 = f32[4,640,11,64]{1,0,3,2:T(4,128)} dynamic-update-slice(f32[4,640,11,64]{1,0,3,2:T(4,128)} %get-tuple-element.1554, f32[1,640,11,64]{1,0,3,2:T(1,128)} %copy.258, s32[]{:T(128)S(6)} %copy.301, s32[]{:T(128)} %constant.225.clone.1..sunk.3, s32[]{:T(128)} %constant.225.clone.1..sunk.3, s32[]{:T(128)} %constant.225.clone.1..sunk.3) | dynamic-update-slice | bytes 3604484 | tf_op jit(solution)/shard_map/while/body/jit(dynamic_update_index_in_dim)/dynamic_update_slice | solution.py:260
  768.0 37.8 %dynamic_update_slice.42 = f32[4,640,12,64]{1,0,3,2:T(4,128)} dynamic-update-slice(f32[4,640,12,64]{1,0,3,2:T(4,128)} %get-tuple-element.1553, f32[1,640,12,64]{1,0,3,2:T(1,128)S(1)} %copy.257, s32[]{:T(128)S(6)} %copy.301, s32[]{:T(128)} %constant.225.clone.1..sunk.3, s32[]{:T(128)} %constant.225.clone.1..sunk.3, s32[]{:T(128)} %constant.225.clone.1..sunk.3) | dynamic-update-slice | bytes 3932164 | tf_op jit(solution)/shard_map/while/body/jit(dynamic_update_index_in_dim)/dynamic_update_slice | solution.py:260
  836.2 28.8 %while.85 = (s32[]{:T(128)}, f32[320,64]{0,1:T(8,128)S(1)}, f32[4,640,64]{1,2,0:T(8,128)S(1)}, s32[320]{0:T(512)S(1)}, s32[4,640]{1,0:T(4,128)S(1)}, /*index=5*/...) while((s32[]{:T(128)}, f32[320,64]{0,1:T(8,128)S(1)}, ...), condition=%wide.region_35.38_spmd.clone, body=%wide.region_32.37_spmd.clone.sunk | while | flops 126669760 | bytes 25789292 | solution.py:316
  922.4 51.1 %reduce-scatter.24.cloned.1.call-done = f32[320,704]{1,0:T(8,128)} async-done(((f32[2560,704]{1,0:T(8,128)}), f32[320,704]{1,0:T(8,128)}) %reduce-scatter.24.cloned.1.call-update) | async-done | bytes 901136
  975.0 71.8 %reduce-scatter.26.cloned.1.call-done = f32[320,768]{1,0:T(8,128)} async-done(((f32[2560,768]{1,0:T(8,128)}), f32[320,768]{1,0:T(8,128)}) %reduce-scatter.26.cloned.1.call-update) | async-done | bytes 983056
  1053.3 44.2 %reduce-scatter.16.cloned.1.call-done = f32[192,768]{1,0:T(8,128)} async-done(((f32[768,768]{1,0:T(8,128)}), f32[192,768]{1,0:T(8,128)}) %reduce-scatter.16.cloned.1.call-update) | async-done | bytes 589840 | tf_op jit(solution)/shard_map/reduce_scatter | solution.py:349
  1097.5 163.2 %reduce-scatter.20.cloned.1.call-done = f32[768,768]{1,0:T(8,128)} async-done(((f32[3072,768]{1,0:T(8,128)}), f32[768,768]{1,0:T(8,128)}) %reduce-scatter.20.cloned.1.call-update) | async-done | bytes 2359312 | tf_op jit(solution)/shard_map/reduce_scatter | solution.py:353
  1260.7 164.4 %reduce-scatter.18.cloned.1.call-done = f32[192,3072]{1,0:T(8,128)} async-done(((f32[768,3072]{1,0:T(8,128)}), f32[192,3072]{1,0:T(8,128)}) %reduce-scatter.18.cloned.1.call-update) | async-done | bytes 2359312 | tf_op jit(solution)/shard_map/reduce_scatter | solution.py:352
  1425.1 126.7 %reduce-scatter.14.cloned.1.call-done = f32[192,2304]{1,0:T(8,128)} async-done(((f32[768,2304]{1,0:T(8,128)}), f32[192,2304]{1,0:T(8,128)}) %reduce-scatter.14.cloned.1.call-update) | async-done | bytes 1769488 | tf_op jit(solution)/shard_map/reduce_scatter | solution.py:348
  1570.3 18.2 %all-reduce.10 = (f32[768]{0:T(1024)S(1)}, f32[768]{0:T(1024)S(1)}, f32[768]{0:T(1024)S(1)}, f32[768]{0:T(1024)S(1)}) all-reduce(f32[768]{0:T(1024)S(1)} %get-tuple-element.830, f32[768]{0:T(1024)S(1)} %get-tuple-element.833, f32[768]{0:T(1024)S(1)} %copy-done.52, ...), channel_id=7, replica_groups=mesh['ctx'=8,'fsdp'=4] {'fsdp'}, use_global_device_ids=true, to_apply=%region_42.45.clone | all-reduce | flops 3072 | bytes 24576
  1604.0 76.0 %all-reduce.14.cloned.1.call-done = (f32[192,2304]{1,0:T(8,128)}, f32[192,768]{1,0:T(8,128)}, f32[192,3072]{1,0:T(8,128)}, f32[768,768]{1,0:T(8,128)}) async-done(((f32[192,2304]{1,0:T(8,128)}, f32[192,768]{1,0:T(8,128)}, f32[192,3072]{1,0:T(8,128)}, f32[768,768]{1,0:T(8,128)}), (f32[192,2304]{1,0:T(8,128)}, f32[192,768]{1,0:T(8,128)}, f32[192,3072]{1,0:T(8,128)}, ...) | async-done | bytes 7077904 | tf_op jit(solution)/shard_map/psum | solution.py:355
  (602 shorter events, 467.1 us)
Async XLA Ops:
  7.2 75.7 %all-gather.11.cloned.1.call-start = ((), (), s32[]{:S(2)}) async-start(), calls=%async_computation.13 | async-start | bytes 4423680 | tf_op jit(solution)/shard_map/all_gather | solution.py:106
  10.3 20.8 %all-to-all-start = ((bf16[8,40,768]{2,1,0:T(8,128)(2,1)}), bf16[8,40,768]{2,1,0:T(8,128)(2,1)S(1)}, u32[]{:S(2)}, u32[]{:S(2)}) async-start(bf16[8,40,768]{2,1,0:T(8,128)(2,1)} %broadcast_select_fusion), calls=%async_computation | async-start | bytes 983040 | tf_op jit(solution)/shard_map/all_to_all | solution.py:118
  15.5 106.1 %all-gather.15.cloned.1.call-start = ((), (), s32[]{:S(2)}) async-start(), calls=%async_computation.15 | async-start | bytes 4423680 | tf_op jit(solution)/shard_map/all_gather | solution.py:128
  87.4 125.2 %all-gather.21.cloned.1.call-start = ((), (), s32[]{:S(2)}) async-start(), calls=%async_computation.18 | async-start | bytes 5898240 | tf_op jit(solution)/shard_map/all_gather | solution.py:111
  88.1 160.9 %all-gather.13.cloned.1.call-start = ((), (), s32[]{:S(2)}) async-start(), calls=%async_computation.14 | async-start | bytes 4423680 | tf_op jit(solution)/shard_map/all_gather | solution.py:129
  88.7 220.1 %all-gather.17.cloned.1.call-start = ((), (), s32[]{:S(2)}) async-start(), calls=%async_computation.16 | async-start | bytes 1474560 | tf_op jit(solution)/shard_map/all_gather | solution.py:107
  89.3 281.6 %all-gather.19.cloned.1.call-start = ((), (), s32[]{:S(2)}) async-start(), calls=%async_computation.17 | async-start | bytes 5898240 | tf_op jit(solution)/shard_map/all_gather | solution.py:110
  149.0 8.4 all-to-all-start.1
  168.0 99.8 %all-to-all-start.2 = ((f32[8,1,2560]{2,1,0:T(1,128)}), f32[8,1,2560]{2,1,0:T(1,128)S(1)}, u32[]{:S(2)}, u32[]{:S(2)}) async-start(f32[8,1,2560]{2,1,0:T(1,128)} %copy.159), calls=%async_computation.2 | async-start | bytes 163840 | tf_op jit(solution)/shard_map/all_to_all | solution.py:183
  806.8 8.8 all-to-all-start.3
  827.6 8.4 all-to-all-start.4
  831.0 90.4 %reduce-scatter.22.cloned.1.call-start = ((), (), s32[]{:S(2)}) async-start(), calls=%async_computation.23 | async-start | bytes 1474560
  866.5 107.0 %reduce-scatter.24.cloned.1.call-start = ((), (), s32[]{:S(2)}) async-start(), calls=%async_computation.24 | async-start | bytes 8847360
  882.1 164.6 %reduce-scatter.26.cloned.1.call-start = ((), (), s32[]{:S(2)}) async-start(), calls=%async_computation.25 | async-start | bytes 8847360
  898.4 199.1 %reduce-scatter.16.cloned.1.call-start = ((), (), s32[]{:S(2)}) async-start(), calls=%async_computation.20 | async-start | bytes 2949120 | tf_op jit(solution)/shard_map/reduce_scatter | solution.py:349
  901.8 358.9 %reduce-scatter.20.cloned.1.call-start = ((), (), s32[]{:S(2)}) async-start(), calls=%async_computation.22 | async-start | bytes 11796480 | tf_op jit(solution)/shard_map/reduce_scatter | solution.py:353
  910.8 514.3 %reduce-scatter.18.cloned.1.call-start = ((), (), s32[]{:S(2)}) async-start(), calls=%async_computation.21 | async-start | bytes 11796480 | tf_op jit(solution)/shard_map/reduce_scatter | solution.py:352
  919.9 631.9 %reduce-scatter.14.cloned.1.call-start = ((), (), s32[]{:S(2)}) async-start(), calls=%async_computation.19 | async-start | bytes 8847360 | tf_op jit(solution)/shard_map/reduce_scatter | solution.py:348
  1053.2 498.5 %copy-start.5 = (bf16[8,40,768]{2,1,0:T(8,128)(2,1)S(1)}, bf16[8,40,768]{2,1,0:T(8,128)(2,1)}, u32[]{:S(2)}) copy-start(bf16[8,40,768]{2,1,0:T(8,128)(2,1)} %copy-done.3) | copy-start | bytes 1474564
  1053.2 498.5 %copy-start.37 = (f32[768]{0:T(1024)S(1)}, f32[768]{0:T(1024)}, u32[]{:S(2)}) copy-start(f32[768]{0:T(1024)} %copy-done.36) | copy-start | bytes 9220
  1053.2 498.5 %copy-start.41 = (f32[320]{0:T(512)S(1)}, f32[320]{0:T(512)}, u32[]{:S(2)}) copy-start(f32[320]{0:T(512)} %copy-done.40) | copy-start | bytes 3844
  1053.2 498.5 %copy-start.43 = (f32[320]{0:T(512)S(1)}, f32[320]{0:T(512)}, u32[]{:S(2)}) copy-start(f32[320]{0:T(512)} %copy-done.42) | copy-start | bytes 3844
  1053.2 626.7 %all-reduce.14.cloned.1.call-start = ((), (), s32[]{:S(2)}) async-start(), calls=%async_computation.26 | async-start | bytes 14155776 | tf_op jit(solution)/shard_map/psum | solution.py:355
  1559.1 43.1 %all-to-all-start.5 = ((f32[8,40,768]{2,1,0:T(8,128)}), f32[8,40,768]{2,1,0:T(8,128)S(1)}, u32[]{:S(2)}, u32[]{:S(2)}) async-start(f32[8,40,768]{2,1,0:T(8,128)} %bitcast.351), calls=%async_computation.5 | async-start | bytes 1966080 | tf_op jit(solution)/shard_map/all_to_all | solution.py:337
  (59 other events, 2809.9 us)
Sparse Core Ops, SparseCore 0:
  9.6 73.2 all-gather.10
  87.5 33.9 all-gather.14
  123.1 89.4 all-gather.20
  214.9 34.0 all-gather.12
  250.4 30.4 all-gather.16
  282.3 88.5 all-gather.18
  866.7 33.8 reduce-scatter.21
  904.0 69.4 reduce-scatter.23
  977.3 69.3 reduce-scatter.25
  1049.5 48.0 reduce-scatter.15
  1099.9 160.7 reduce-scatter.19
  1262.9 162.1 reduce-scatter.17
  1427.4 124.3 reduce-scatter.13
  1555.3 124.6 all-reduce.13
where the time goes:
time: 1710 us; the launch traced here: 1690 us
  waiting for transfers between devices  925 us (54%)
  local copies, waits for them, and re-layouts  436 us (25%)
  matrix products  184 us (11%)
  blocking collectives  60.9 us (4%)
  other arithmetic  45.2 us (3%)
  starting transfers between devices  23.6 us (1%)
    dynamic_update_slice x16, local copies, waits for them, and re-layouts, body(): lax.scan(phase_main, jnp.zeros((row_count, HEADS - 1, HEAD), jnp.float32)...  311 us
    reduce_scatter x1, waiting for transfers between devices, body(): lax.psum_scatter(grad_up, 'fsdp', scatter_dimension=0, tiled=True)  164 us
    reduce_scatter x1, waiting for transfers between devices, body(): lax.psum_scatter(grad_down, 'fsdp', scatter_dimension=0, tiled=True)  163 us
    reduce_scatter x1, waiting for transfers between devices, body(): lax.psum_scatter(grad_triple, 'fsdp', scatter_dimension=0, tiled=True)  127 us
    unnamed x17, waiting for transfers between devices  126 us
    psum x1, waiting for transfers between devices, body(): lax.psum((shard_g1, shard_b1, shard_triple, shard_output, shard_g2, shard...  76 us
    unnamed x152, local copies, waits for them, and re-layouts  62.8 us
    all_gather x1, waiting for transfers between devices, body(): lax.all_gather(up_weight, 'fsdp', axis=0, tiled=True)  58.7 us
  transfers between devices with their start and end apart: 20, of which 15 were waited for; matrix products, arithmetic and copies ran while one was open for 11% of the time, Pallas kernels for 0%

commit v1 on v0

v1 whole, which is shorter than its diff:
```python
import functools
import math

import jax
import jax.numpy as jnp
from jax import lax
from jax.experimental import pallas as pl
from jax.experimental.pallas import tpu as pltpu
from jax.sharding import PartitionSpec as P

HEADS = 12
HEAD = 64
EPS = 1e-05
FAR = 1e30
SIDE = 128
VMEM_LIMIT = 60 * 1024 * 1024


def layer_norm(values, gain_vec, offset):
    center = values - jnp.mean(values, axis=-1, keepdims=True)
    spread = jnp.mean(center * center, axis=-1, keepdims=True)
    return center * lax.rsqrt(spread + EPS) * gain_vec + offset


def norm_back(values, gain_vec, grad_vec):
    center = values - jnp.mean(values, axis=-1, keepdims=True)
    spread = jnp.mean(center * center, axis=-1, keepdims=True)
    inv = lax.rsqrt(spread + EPS)
    unit = center * inv
    scaled = grad_vec * gain_vec
    mean_a = jnp.mean(scaled, axis=-1, keepdims=True)
    mean_b = jnp.mean(scaled * unit, axis=-1, keepdims=True)
    grad_in = inv * (scaled - mean_a - unit * mean_b)
    return grad_in, jnp.sum(grad_vec * unit, axis=0), jnp.sum(grad_vec, axis=0)


def gelu_back(values, grad_vec):
    unused, pullback = jax.vjp(jax.nn.gelu, values)
    return pullback(grad_vec)[0]


def matmul(left_side, right_side):
    return jnp.dot(left_side, right_side, preferred_element_type=jnp.float32)


def dot_tn(left_side, right_side):
    return lax.dot_general(
        left_side, right_side, (((0,), (0,)), ((), ())), preferred_element_type=jnp.float32
    )


def dot_nt(left_side, right_side):
    return lax.dot_general(
        left_side, right_side, (((1,), (1,)), ((), ())), preferred_element_type=jnp.float32
    )


class Plan:
    def __init__(self, row_count, n_ctx, n_seq, width):
        self.rows = row_count
        self.blocks = n_ctx
        self.part = row_count // n_ctx
        self.keys = row_count * n_ctx
        self.seqs = n_seq
        self.width = width
        self.small = self.keys <= 4096
        self.heads = 6 if self.small else 2
        self.groups = HEADS // self.heads
        self.step_groups = self.groups if self.small else 1
        self.steps = self.groups // self.step_groups
        self.span = self.heads * HEAD
        self.step_span = self.step_groups * self.span
        self.live = self.heads * self.part
        self.lanes = -(-(self.live + 1) // 128) * 128
        self.pairs = n_ctx * (n_ctx + 1) // 2
        self.part_pad = -(-self.part // 8) * 8


def scalar_start(plan, meta, position):
    start, end = 0, 0
    for n in range(plan.seqs):
        length = meta[n]
        end = end + length
        start = start + jnp.where(position >= end, length, 0)
    return start


def lane_parts(plan):
    lane = lax.broadcasted_iota(jnp.int32, (1, plan.lanes), 1)
    head = jnp.zeros_like(lane)
    for k in range(1, plan.heads):
        head = head + (lane >= k * plan.part).astype(jnp.int32)
    return lane, head, lane - head * plan.part


def block_copies(plan, step, t, kv, kb, vb, qk, sem):
    rows = pl.ds(pl.multiple_of(t * plan.rows, 8), plan.rows)
    k_at = pl.multiple_of(step * plan.step_span, 128)
    v_at = pl.multiple_of(plan.width + step * plan.step_span, 128)
    return (
        pltpu.make_async_copy(kv.at[rows, pl.ds(k_at, plan.step_span)], kb.at[t], sem.at[0, t]),
        pltpu.make_async_copy(kv.at[rows, pl.ds(v_at, plan.step_span)], vb.at[t], sem.at[1, t]),
        pltpu.make_async_copy(
            kv.at[rows, pl.ds(2 * plan.width, SIDE)], qk.at[t, :, pl.ds(0, SIDE)], sem.at[2, t]
        ),
        pltpu.make_async_copy(
            kv.at[rows, pl.ds(0, SIDE)], qk.at[t, :, pl.ds(SIDE, SIDE)], sem.at[3, t]
        ),
    )


def part_setup(plan, meta, s):
    lane, head, row = lane_parts(plan)
    offset = meta[plan.seqs + s] * plan.part
    first = s * plan.rows + offset
    pos = first + row
    start = scalar_start(plan, meta, pos)
    query = lax.broadcasted_iota(jnp.int32, (plan.rows, 1), 0)
    earlier = (query < offset + row) | (lane >= plan.live)
    block_pos = s * plan.rows + lax.broadcasted_iota(jnp.int32, (1, plan.rows), 1)
    return dict(
        lane=lane,
        pos=pos,
        start=start,
        earlier=earlier.astype(jnp.bfloat16),
        block_pos=block_pos,
        block_start=scalar_start(plan, meta, block_pos),
        select_from=scalar_start(plan, meta, s * plan.rows) // plan.rows,
        attend_from=scalar_start(plan, meta, first) // plan.rows,
    )


def masked_prior(plan, info, s, t, qk, acc):
    key = t * plan.rows + lax.broadcasted_iota(jnp.int32, (plan.rows, 1), 0)
    first = dot_nt(qk[t, :, SIDE : SIDE + HEAD], qk[s, :, :HEAD])
    chosen = (key < info["block_pos"]) & (key > info["block_start"])
    select = jnp.where(chosen, jnp.maximum(first, 0.0), 0.0)
    high = select.astype(jnp.bfloat16)
    rest = select - high.astype(jnp.float32)
    mid = rest.astype(jnp.bfloat16)
    low = (rest - mid.astype(jnp.float32)).astype(jnp.bfloat16)
    earlier = info["earlier"]
    sums = matmul(high, earlier) + matmul(mid, earlier) + matmul(low, earlier)
    before = acc[t]
    prior = before + sums
    acc[t] = before + jnp.broadcast_to(sums[:, plan.live : plan.live + 1], sums.shape)
    allowed = (key <= info["pos"]) & (key >= info["start"]) & (info["lane"] < plan.live)
    return jnp.where(allowed, prior, FAR)


def spread_rows(plan, rows_value, copies, own_head):
    return jnp.where(own_head, dot_tn(rows_value, copies), 0.0)


def head_masks(plan):
    lane, head, row = lane_parts(plan)
    live = lane < plan.live
    column_head = lax.broadcasted_iota(jnp.int32, (plan.span, 1), 0) // HEAD
    own_head = (column_head == head) & live
    copies = (lax.broadcasted_iota(jnp.int32, (plan.part, 1), 0) == row) & live
    return own_head, copies.astype(jnp.bfloat16)


def attend_kernel(
    plan, meta, q_ref, kv, high_ref, low_ref, total_ref, kb, vb, qk, vt, qbd, numer, total, acc, sem
):
    step = pl.program_id(0)

    def begin(t, carry):
        for copy in block_copies(plan, step, t, kv, kb, vb, qk, sem):
            copy.start()
        return carry

    lax.fori_loop(0, plan.blocks, begin, 0)
    own_head, copies = head_masks(plan)
    acc[...] = jnp.zeros_like(acc)

    def one_part(s, carry):
        for copy in block_copies(plan, step, s, kv, kb, vb, qk, sem):
            copy.wait()
        vt[s] = vb[s].T
        info = part_setup(plan, meta, s)
        q_part = q_ref[s]
        for g in range(plan.step_groups):
            cols = slice(g * plan.span, (g + 1) * plan.span)
            qbd[g] = spread_rows(plan, q_part[:, cols], copies, own_head).astype(jnp.bfloat16)
        numer[...] = jnp.zeros_like(numer)
        total[...] = jnp.zeros_like(total)

        def tile(t, carry):
            prior = masked_prior(plan, info, s, t, qk, acc)

            @pl.when(t >= info["attend_from"])
            def _():
                for g in range(plan.step_groups):
                    cols = slice(g * plan.span, (g + 1) * plan.span)
                    logits = matmul(kb[t, :, cols], qbd[g])
                    expo = jnp.exp(logits - prior)
                    total[g] += jnp.sum(expo.reshape(plan.rows // 8, 8, plan.lanes), axis=0)
                    numer[g] += matmul(vt[t, cols, :], expo.astype(jnp.bfloat16))

            return carry

        lax.fori_loop(info["select_from"], s + 1, tile, 0)
        for g in range(plan.step_groups):
            cols = slice(g * plan.span, (g + 1) * plan.span)
            whole = jnp.sum(total[g], axis=0, keepdims=True)
            whole = jnp.where(info["lane"] < plan.live, whole, 1.0)
            mixed = jnp.where(own_head, numer[g] / whole, 0.0)
            high = mixed.astype(jnp.bfloat16)
            low = (mixed - high.astype(jnp.float32)).astype(jnp.bfloat16)
            high_ref[s, :, cols] = dot_nt(copies, high).astype(jnp.bfloat16)
            low_ref[s, :, cols] = dot_nt(copies, low).astype(jnp.bfloat16)
            total_ref[0, g, pl.ds(s, 1), :] = whole
        return carry

    lax.fori_loop(0, plan.blocks, one_part, 0)


def attend(plan, meta, queries, kv):
    part_block = pl.BlockSpec((plan.blocks, plan.part, plan.step_span), lambda i, m: (0, 0, i))
    out = jax.ShapeDtypeStruct((plan.blocks, plan.part, plan.width), jnp.bfloat16)
    sg, nb = plan.step_groups, plan.blocks
    return pl.pallas_call(
        functools.partial(attend_kernel, plan),
        name="attend",
        grid_spec=pltpu.PrefetchScalarGridSpec(
            num_scalar_prefetch=1,
            grid=(plan.steps,),
            in_specs=[part_block, pl.BlockSpec(memory_space=pl.ANY)],
            out_specs=[
                part_block,
                part_block,
                pl.BlockSpec((1, sg, nb, plan.lanes), lambda i, m: (i, 0, 0, 0)),
            ],
            scratch_shapes=[
                pltpu.VMEM((nb, plan.rows, plan.step_span), jnp.bfloat16),
                pltpu.VMEM((nb, plan.rows, plan.step_span), jnp.bfloat16),
                pltpu.VMEM((nb, plan.rows, 2 * SIDE), jnp.bfloat16),
                pltpu.VMEM((nb, plan.step_span, plan.rows), jnp.bfloat16),
                pltpu.VMEM((sg, plan.span, plan.lanes), jnp.bfloat16),
                pltpu.VMEM((sg, plan.span, plan.lanes), jnp.float32),
                pltpu.VMEM((sg, 8, plan.lanes), jnp.float32),
                pltpu.VMEM((nb, plan.rows, plan.lanes), jnp.float32),
                pltpu.SemaphoreType.DMA((4, nb)),
            ],
        ),
        out_shape=[
            out,
            out,
            jax.ShapeDtypeStruct((plan.steps, sg, nb, plan.lanes), jnp.float32),
        ],
        compiler_params=pltpu.CompilerParams(vmem_limit_bytes=VMEM_LIMIT),
        cost_estimate=pl.CostEstimate(
            flops=4 * plan.rows * plan.keys * plan.width,
            bytes_accessed=4 * plan.keys * plan.width,
            transcendentals=plan.rows * plan.keys * HEADS,
        ),
    )(meta, queries.reshape(plan.blocks, plan.part, plan.width), kv)


def split_two(value):
    high = value.astype(jnp.bfloat16)
    return high, (value - high.astype(jnp.float32)).astype(jnp.bfloat16)


def back_kernel(
    plan,
    meta,
    q_ref,
    gm_ref,
    high_ref,
    low_ref,
    total_ref,
    kv,
    dq_ref,
    dk_ref,
    dv_ref,
    within_ref,
    sums_ref,
    kb,
    vb,
    qk,
    kt,
    qbd,
    sbd,
    ratio,
    dq,
    dk,
    dv,
    acc,
    stage,
    sem,
    out_sem,
):
    step = pl.program_id(0)

    def begin(t, carry):
        for copy in block_copies(plan, step, t, kv, kb, vb, qk, sem):
            copy.start()
        return carry

    lax.fori_loop(0, plan.blocks, begin, 0)
    own_head, copies = head_masks(plan)
    acc[...] = jnp.zeros_like(acc)
    dk[...] = jnp.zeros_like(dk)
    dv[...] = jnp.zeros_like(dv)

    @pl.when(step == 0)
    def _():
        sums_ref[...] = jnp.zeros_like(sums_ref)

    side_lane = lax.broadcasted_iota(jnp.int32, (1, SIDE), 1)

    def one_part(s, carry):
        for copy in block_copies(plan, step, s, kv, kb, vb, qk, sem):
            copy.wait()
        kt[s] = kb[s].T
        info = part_setup(plan, meta, s)
        q_part, gm_part = q_ref[s], gm_ref[s]
        high_part, low_part = high_ref[s], low_ref[s]
        for g in range(plan.step_groups):
            cols = slice(g * plan.span, (g + 1) * plan.span)
            whole = total_ref[0, g, pl.ds(s, 1), :]
            qbd[g] = spread_rows(plan, q_part[:, cols], copies, own_head).astype(jnp.bfloat16)
            gm_high, gm_low = split_two(gm_part[:, cols])
            grad = spread_rows(plan, gm_high, copies, own_head) + spread_rows(
                plan, gm_low, copies, own_head
            )
            mixed = spread_rows(plan, high_part[:, cols], copies, own_head) + spread_rows(
                plan, low_part[:, cols], copies, own_head
            )
            sbd[g] = (grad / whole).astype(jnp.bfloat16)
            ratio[g] = jnp.broadcast_to(
                jnp.sum(grad * mixed, axis=0, keepdims=True) / whole, (8, plan.lanes)
            )
        dq[...] = jnp.zeros_like(dq)
        lane_row = lax.broadcasted_iota(jnp.int32, (plan.lanes, 1), 0)
        row_at = lane_row
        for k in range(1, plan.heads):
            row_at = row_at - jnp.where(lane_row >= k * plan.part, plan.part, 0)
        fold = ((row_at > side_lane) & (side_lane < plan.part)) | (side_lane == plan.part + s)
        fold = jnp.where(fold & (lane_row < plan.live), -1.0, 0.0).astype(jnp.bfloat16)

        def tile(t, carry):
            prior = masked_prior(plan, info, s, t, qk, acc)

            @pl.when(t >= info["attend_from"])
            def _():
                within = jnp.zeros((plan.rows, SIDE), jnp.float32)
                for g in range(plan.step_groups):
                    cols = slice(g * plan.span, (g + 1) * plan.span)
                    logits = matmul(kb[t, :, cols], qbd[g])
                    expo = jnp.exp(logits - prior)
                    back = matmul(vb[t, :, cols], sbd[g])
                    gz = expo * (back - ratio[g, 0:1, :])
                    gz_high, gz_low = split_two(gz)
                    dv[t, :, cols] += dot_nt(expo.astype(jnp.bfloat16), sbd[g])
                    dk[t, :, cols] += dot_nt(gz_high, qbd[g])
                    dq[g] += matmul(kt[t, cols, :], gz_high)
                    within = within + matmul(gz_high, fold) + matmul(gz_low, fold)
                sums_ref[t] += jnp.where(side_lane < plan.part, 0.0, within)
                put_within(plan, within, s, t, within_ref, stage, out_sem)

            return carry

        lax.fori_loop(info["select_from"], s + 1, tile, 0)
        for g in range(plan.step_groups):
            cols = slice(g * plan.span, (g + 1) * plan.span)
            value = jnp.where(own_head, dq[g] * (1.0 / math.sqrt(HEAD)), 0.0)
            high, low = split_two(value)
            dq_ref[s, :, cols] = dot_nt(copies, high) + dot_nt(copies, low)
        return carry

    lax.fori_loop(0, plan.blocks, one_part, 0)

    def flush(t, carry):
        dk_ref[t] = dk[t].astype(jnp.bfloat16)
        dv_ref[t] = dv[t].astype(jnp.bfloat16)
        return carry

    lax.fori_loop(0, plan.blocks, flush, 0)


def pair_at(s, t):
    return s * (s + 1) // 2 + t


def put_within(plan, within, s, t, within_ref, stage, out_sem):
    if plan.small:
        within_ref[pair_at(s, t)] = within
        return
    stage[...] = within.T[: plan.part_pad, :]
    copy = pltpu.make_async_copy(stage, within_ref.at[pl.program_id(0), pair_at(s, t)], out_sem)
    copy.start()
    copy.wait()


def attend_back(plan, meta, queries, grad_mixed, high, low, total, kv):
    sg, nb = plan.step_groups, plan.blocks
    part_block = pl.BlockSpec((nb, plan.part, plan.step_span), lambda i, m: (0, 0, i))
    key_block = pl.BlockSpec((nb, plan.rows, plan.step_span), lambda i, m: (0, 0, i))
    pair_shape = (plan.pairs, plan.rows, SIDE)
    if plan.small:
        within_spec = pl.BlockSpec(pair_shape, lambda i, m: (0, 0, 0))
        within_shape = jax.ShapeDtypeStruct(pair_shape, jnp.float32)
    else:
        within_spec = pl.BlockSpec(memory_space=pl.ANY)
        pair_shape = (plan.steps, plan.pairs, plan.part_pad, plan.rows)
        within_shape = jax.ShapeDtypeStruct(pair_shape, jnp.float32)
    out = pl.pallas_call(
        functools.partial(back_kernel, plan),
        name="attend_back",
        grid_spec=pltpu.PrefetchScalarGridSpec(
            num_scalar_prefetch=1,
            grid=(plan.steps,),
            in_specs=[part_block] * 4
            + [
                pl.BlockSpec((1, sg, nb, plan.lanes), lambda i, m: (i, 0, 0, 0)),
                pl.BlockSpec(memory_space=pl.ANY),
            ],
            out_specs=[
                part_block,
                key_block,
                key_block,
                within_spec,
                pl.BlockSpec((nb, plan.rows, SIDE), lambda i, m: (0, 0, 0)),
            ],
            scratch_shapes=[
                pltpu.VMEM((nb, plan.rows, plan.step_span), jnp.bfloat16),
                pltpu.VMEM((nb, plan.rows, plan.step_span), jnp.bfloat16),
                pltpu.VMEM((nb, plan.rows, 2 * SIDE), jnp.bfloat16),
                pltpu.VMEM((nb, plan.step_span, plan.rows), jnp.bfloat16),
                pltpu.VMEM((sg, plan.span, plan.lanes), jnp.bfloat16),
                pltpu.VMEM((sg, plan.span, plan.lanes), jnp.bfloat16),
                pltpu.VMEM((sg, 8, plan.lanes), jnp.float32),
                pltpu.VMEM((sg, plan.span, plan.lanes), jnp.float32),
                pltpu.VMEM((nb, plan.rows, plan.step_span), jnp.float32),
                pltpu.VMEM((nb, plan.rows, plan.step_span), jnp.float32),
                pltpu.VMEM((nb, plan.rows, plan.lanes), jnp.float32),
                pltpu.VMEM((plan.part_pad, plan.rows), jnp.float32),
                pltpu.SemaphoreType.DMA((4, nb)),
                pltpu.SemaphoreType.DMA,
            ],
        ),
        out_shape=[
            jax.ShapeDtypeStruct((nb, plan.part, plan.width), jnp.float32),
            jax.ShapeDtypeStruct((nb, plan.rows, plan.width), jnp.bfloat16),
            jax.ShapeDtypeStruct((nb, plan.rows, plan.width), jnp.bfloat16),
            within_shape,
            jax.ShapeDtypeStruct((nb, plan.rows, SIDE), jnp.float32),
        ],
        compiler_params=pltpu.CompilerParams(vmem_limit_bytes=VMEM_LIMIT),
        cost_estimate=pl.CostEstimate(
            flops=10 * plan.rows * plan.keys * plan.width,
            bytes_accessed=12 * plan.keys * plan.width,
            transcendentals=plan.rows * plan.keys * HEADS,
        ),
    )(
        meta,
        queries.reshape(nb, plan.part, plan.width),
        grad_mixed.reshape(nb, plan.part, plan.width),
        high,
        low,
        total,
        kv,
    )
    return out


def first_kernel(plan, meta, q_ref, k_ref, later_ref, within_ref, dq_ref, dk_ref, stage, sem):
    dk_ref[...] = jnp.zeros_like(dk_ref)
    side_lane = lax.broadcasted_iota(jnp.int32, (1, SIDE), 1)
    row = lax.broadcasted_iota(jnp.int32, (1, plan.part), 1)

    def one_part(s, carry):
        first = s * plan.rows + meta[plan.seqs + s] * plan.part
        pos = first + row
        start = scalar_start(plan, meta, pos)
        attend_from = scalar_start(plan, meta, first) // plan.rows
        q_part = q_ref[s, :, :HEAD]

        def tile(t, total):
            k_tile = k_ref[pl.ds(pl.multiple_of(t * plan.rows, 8), plan.rows), :HEAD]
            key = t * plan.rows + lax.broadcasted_iota(jnp.int32, (plan.rows, 1), 0)
            logits = dot_nt(k_tile, q_part)
            chosen = (key < pos) & (key > start) & (logits > 0.0)
            if plan.small:
                within = within_ref[pair_at(s, t)]
            else:
                within = jnp.zeros((plan.part_pad, plan.rows), jnp.float32)
                for g in range(plan.steps):
                    copy = pltpu.make_async_copy(within_ref.at[g, pair_at(s, t)], stage, sem)
                    copy.start()
                    copy.wait()
                    within = within + stage[...]
                empty = jnp.zeros((SIDE - plan.part_pad, plan.rows), jnp.float32)
                within = jnp.concatenate([within, empty], axis=0).T
            later = jnp.sum(
                jnp.where(side_lane == s, later_ref[t], 0.0), axis=1, keepdims=True
            )
            extra = jnp.where(chosen, within[:, : plan.part] + later, 0.0).astype(jnp.bfloat16)
            dk_ref[t] += jnp.concatenate(
                [matmul(extra, q_part), jnp.zeros((plan.rows, SIDE - HEAD), jnp.float32)], axis=1
            )
            return total + dot_tn(extra, k_tile)

        total = lax.fori_loop(
            attend_from, s + 1, tile, jnp.zeros((plan.part, HEAD), jnp.float32)
        )
        dq_ref[s] = jnp.concatenate(
            [
                total * (1.0 / math.sqrt(HEAD)),
                jnp.zeros((plan.part, SIDE - HEAD), jnp.float32),
            ],
            axis=1,
        )
        return carry

    lax.fori_loop(0, plan.blocks, one_part, 0)


def first_head(plan, meta, queries, kv, later, within):
    nb = plan.blocks
    if plan.small:
        within_spec = pl.BlockSpec(within.shape, lambda i, m: (0, 0, 0))
    else:
        within_spec = pl.BlockSpec(memory_space=pl.ANY)
    return pl.pallas_call(
        functools.partial(first_kernel, plan),
        name="first_head",
        grid_spec=pltpu.PrefetchScalarGridSpec(
            num_scalar_prefetch=1,
            grid=(1,),
            in_specs=[
                pl.BlockSpec((nb, plan.part, SIDE), lambda i, m: (0, 0, 0)),
                pl.BlockSpec((plan.keys, SIDE), lambda i, m: (0, 0)),
                pl.BlockSpec((nb, plan.rows, SIDE), lambda i, m: (0, 0, 0)),
                within_spec,
            ],
            out_specs=[
                pl.BlockSpec((nb, plan.part, SIDE), lambda i, m: (0, 0, 0)),
                pl.BlockSpec((nb, plan.rows, SIDE), lambda i, m: (0, 0, 0)),
            ],
            scratch_shapes=[
                pltpu.VMEM((plan.part_pad, plan.rows), jnp.float32),
                pltpu.SemaphoreType.DMA,
            ],
        ),
        out_shape=[
            jax.ShapeDtypeStruct((nb, plan.part, SIDE), jnp.float32),
            jax.ShapeDtypeStruct((nb, plan.rows, SIDE), jnp.float32),
        ],
        compiler_params=pltpu.CompilerParams(vmem_limit_bytes=VMEM_LIMIT),
        cost_estimate=pl.CostEstimate(
            flops=6 * plan.rows * plan.keys * HEAD,
            bytes_accessed=1024 * plan.keys,
            transcendentals=0,
        ),
    )(meta, queries.reshape(nb, plan.part, plan.width), kv, later, within)


def body(
    tokens,
    lengths,
    deal_table,
    norm_one_gain,
    norm_one_bias,
    triple_weight,
    output_weight,
    norm_two_gain,
    norm_two_bias,
    up_weight,
    down_weight,
    cotangent,
):
    bf16, f32 = jnp.bfloat16, jnp.float32
    n_ctx = lax.axis_size("ctx")
    device = lax.axis_index("ctx")
    row_count, width = tokens.shape
    plan = Plan(row_count, n_ctx, lengths.shape[1], width)
    part_rows = plan.part
    head_scale = 1.0 / math.sqrt(HEAD)
    route_table = deal_table[0]
    counter = jnp.arange(n_ctx, dtype=jnp.int32)
    route_hits = route_table[:, :, None] == counter[None, None, :]
    inverse = jnp.sum(jnp.where(route_hits, counter[None, :, None], 0), axis=1)
    my_parts = jnp.take(inverse, device, axis=0)
    my_slots = jnp.take(inverse, device, axis=1)
    my_owners = jnp.take(route_table, device, axis=0)
    part_first = counter[:, None] * row_count + inverse * part_rows
    my_first = counter * row_count + my_slots * part_rows
    meta = jnp.concatenate([lengths[0], my_slots])

    gain_one, bias_one, triple_full, output_full, gain_two, bias_two, up_full, down_full = (
        lax.all_gather(norm_one_gain, "fsdp", axis=0, tiled=True),
        lax.all_gather(norm_one_bias, "fsdp", axis=0, tiled=True),
        lax.all_gather(triple_weight, "fsdp", axis=0, tiled=True),
        lax.all_gather(output_weight, "fsdp", axis=0, tiled=True),
        lax.all_gather(norm_two_gain, "fsdp", axis=0, tiled=True),
        lax.all_gather(norm_two_bias, "fsdp", axis=0, tiled=True),
        lax.all_gather(up_weight, "fsdp", axis=0, tiled=True),
        lax.all_gather(down_weight, "fsdp", axis=0, tiled=True),
    )
    gain_one = gain_one.astype(f32)
    bias_one = bias_one.astype(f32)
    gain_two = gain_two.astype(f32)
    bias_two = bias_two.astype(f32)

    outgoing = jnp.take(tokens.reshape(n_ctx, part_rows, width), my_parts, axis=0)
    dealt = lax.all_to_all(outgoing, "ctx", split_axis=0, concat_axis=0, tiled=True).reshape(
        row_count, width
    )
    natural = tokens.astype(f32)
    resid = dealt.astype(f32)
    hidden_nat = layer_norm(natural, gain_one, bias_one).astype(bf16)
    hidden_one = layer_norm(resid, gain_one, bias_one).astype(bf16)
    kv_part = matmul(hidden_nat, triple_full[:, width:]).astype(bf16)
    side_part = (matmul(hidden_nat, triple_full[:, :SIDE]).astype(bf16) * head_scale).astype(bf16)
    queries = (matmul(hidden_one, triple_full[:, :width]).astype(bf16) * head_scale).astype(bf16)
    kv = lax.all_gather(
        jnp.concatenate([kv_part, side_part], axis=1), "ctx", axis=0, tiled=True
    )

    high, low, total = attend(plan, meta, queries, kv)
    mixed_low = high.reshape(row_count, width)
    middle = resid + matmul(mixed_low, output_full)
    hidden_two = layer_norm(middle, gain_two, bias_two).astype(bf16)
    raised = matmul(hidden_two, up_full)
    activated = jax.nn.gelu(raised).astype(bf16)
    result = (middle + matmul(activated, down_full)).astype(bf16)
    grad_final = cotangent.astype(f32)
    grad_down = dot_tn(activated, cotangent).astype(bf16)
    grad_raised = gelu_back(raised, dot_nt(cotangent, down_full)).astype(bf16)
    grad_up = dot_tn(hidden_two, grad_raised).astype(bf16)
    grad_hidden_two = dot_nt(grad_raised, up_full)
    grad_mid_norm, grad_gain_two, grad_bias_two = norm_back(middle, gain_two, grad_hidden_two)
    grad_middle = grad_final + grad_mid_norm
    grad_attended = grad_middle.astype(bf16)
    grad_output = dot_tn(mixed_low, grad_attended).astype(bf16)
    grad_mixed = dot_nt(grad_attended, output_full)

    dq, dk, dv, within, sums = attend_back(
        plan, meta, queries, grad_mixed, high, low, total, kv
    )
    sums = sums.reshape(plan.keys, SIDE)[:, part_rows : part_rows + n_ctx]
    all_sums = lax.all_gather(sums.T, "ctx", axis=0, tiled=False)
    order = inverse.T * part_rows + counter[None, :] * row_count
    is_later = order.reshape(-1)[:, None] > my_first[None, :]
    is_later = jnp.pad(is_later.astype(f32), ((0, 0), (0, SIDE - n_ctx)))
    later = lax.dot_general(
        all_sums.reshape(n_ctx * n_ctx, plan.keys),
        is_later,
        (((0,), (0,)), ((), ())),
        precision=lax.Precision.HIGHEST,
        preferred_element_type=f32,
    ).reshape(n_ctx, row_count, SIDE)
    dq_extra, dk_extra = first_head(plan, meta, queries, kv, later, within)

    key_sum = lax.psum_scatter(
        dk.reshape(plan.keys, width), "ctx", scatter_dimension=0, tiled=True
    )
    value_sum = lax.psum_scatter(
        dv.reshape(plan.keys, width), "ctx", scatter_dimension=0, tiled=True
    )
    extra_sum = lax.psum_scatter(
        dk_extra.reshape(plan.keys, SIDE), "ctx", scatter_dimension=0, tiled=True
    )
    grad_q = dq.reshape(row_count, width) + jnp.pad(
        dq_extra.reshape(row_count, SIDE), ((0, 0), (0, width - SIDE))
    )
    grad_q = grad_q.astype(bf16)
    grad_key = key_sum.astype(f32) + jnp.pad(extra_sum, ((0, 0), (0, width - SIDE)))
    grad_kv = jnp.concatenate([grad_key.astype(bf16), value_sum], axis=1)

    back_q = dot_nt(grad_q, triple_full[:, :width])
    dealt_in, gain_a, bias_a = norm_back(resid, gain_one, back_q)
    grad_dealt = (grad_middle + dealt_in).astype(bf16)
    returned = lax.all_to_all(
        grad_dealt.reshape(n_ctx, part_rows, width), "ctx", split_axis=0, concat_axis=0, tiled=True
    )
    returned = jnp.take(returned, my_owners, axis=0).reshape(row_count, width)
    back_kv = dot_nt(grad_kv, triple_full[:, width:])
    natural_in, gain_b, bias_b = norm_back(natural, gain_one, back_kv)
    token_grad = returned.astype(f32) + natural_in
    grad_triple = jnp.concatenate(
        [dot_tn(hidden_one, grad_q), dot_tn(hidden_nat, grad_kv)], axis=1
    ).astype(bf16)

    shard_triple, shard_output, shard_up, shard_down = (
        lax.psum_scatter(grad_triple, "fsdp", scatter_dimension=0, tiled=True),
        lax.psum_scatter(grad_output, "fsdp", scatter_dimension=0, tiled=True),
        lax.psum_scatter(grad_up, "fsdp", scatter_dimension=0, tiled=True),
        lax.psum_scatter(grad_down, "fsdp", scatter_dimension=0, tiled=True),
    )
    sum_triple, sum_output, sum_up, sum_down = lax.psum(
        (shard_triple, shard_output, shard_up, shard_down), "ctx"
    )
    vectors = lax.psum(
        jnp.stack([gain_a + gain_b, bias_a + bias_b, grad_gain_two, grad_bias_two]),
        ("ctx", "fsdp"),
    )
    slot = width // lax.axis_size("fsdp")
    vectors = lax.dynamic_slice_in_dim(vectors, lax.axis_index("fsdp") * slot, slot, axis=1)
    return (
        result,
        token_grad,
        vectors[0],
        vectors[1],
        sum_triple.astype(f32),
        sum_output.astype(f32),
        vectors[2],
        vectors[3],
        sum_up.astype(f32),
        sum_down.astype(f32),
    )


def solution(mesh):
    rows = P(("ctx", "fsdp"), None)
    shard = P("fsdp")
    matrix = P("fsdp", None)
    return jax.shard_map(
        body,
        mesh=mesh,
        in_specs=(
            rows,
            matrix,
            P("fsdp", None, None),
            shard,
            shard,
            matrix,
            matrix,
            shard,
            shard,
            matrix,
            matrix,
            rows,
        ),
        out_specs=(rows, rows, shard, shard, matrix, matrix, shard, shard, matrix, matrix),
        check_vma=False,
    )
```

time: 1710 us -> 977 us (0.57); the launches traced: 1690 us -> 980 us
  local copies, waits for them, and re-layouts: 436 us -> 17.5 us
  waiting for transfers between devices: 925 us -> 657 us
  Pallas kernels: 0 us -> 127 us
  matrix products: 184 us -> 62.8 us
  other arithmetic: 45.2 us -> 23.6 us
    dynamic_update_slice x20 -> x0, local copies, waits for them, and re-layouts: 311 us -> none  [the longest x16 311 us: body(): lax.scan(phase_main, jnp.zeros((row_count, HEADS - 1, HEAD), jnp.float32)...]
    pallas_call x0 -> x3, Pallas kernels: none -> 127 us  [the longest x1 66.9 us: attend_back(): pl.pallas_call(functools.partial(back_kernel, plan), name='attend_back',...]
    dot_general x52 -> x11, matrix products: 161 us -> 38.1 us  [the longest x5 21 us: dot_tn(): lax.dot_general(left_side, right_side, (((0,), (0,)), ((), ())), preferre...]
    unnamed x17 -> x13, waiting for transfers between devices: 126 us -> 3.93 us
    reduce_scatter x0 -> x3, waiting for transfers between devices: none -> 120 us  [the longest x1 53.6 us: body(): lax.psum_scatter(dk.reshape(plan.keys, width), 'ctx', scatter_dimension=0...]
    reduce_scatter x1, waiting for transfers between devices: 163 us -> 86.1 us  [body(): lax.psum_scatter(grad_down, 'fsdp', scatter_dimension=0, tiled=True)]
    reduce_scatter x1, waiting for transfers between devices: 164 us -> 88.1 us  [body(): lax.psum_scatter(grad_up, 'fsdp', scatter_dimension=0, tiled=True)]
    reduce_scatter x1, waiting for transfers between devices: 127 us -> 69.1 us  [body(): lax.psum_scatter(grad_triple, 'fsdp', scatter_dimension=0, tiled=True)]
  transfers between devices with their start and end apart: 20 -> 15, of which waited for: 15 -> 13; matrix products, arithmetic and copies ran while one was open for 11% -> 7% of each run, Pallas kernels for 0% -> 5%
where the time goes in v1:
time: 977 us; the launch traced here: 980 us
  waiting for transfers between devices  657 us (67%)
  Pallas kernels  127 us (13%)
  blocking collectives  69 us (7%)
  matrix products  62.8 us (6%)
  other arithmetic  23.6 us (2%)
  local copies, waits for them, and re-layouts  17.5 us (2%)
  between operations  15.1 us (2%)
    reduce_scatter x1, waiting for transfers between devices, body(): lax.psum_scatter(grad_up, 'fsdp', scatter_dimension=0, tiled=True)  88.1 us
    reduce_scatter x1, waiting for transfers between devices, body(): lax.psum_scatter(grad_down, 'fsdp', scatter_dimension=0, tiled=True)  86.1 us
    all_gather x1, waiting for transfers between devices, body(): lax.all_gather(up_weight, 'fsdp', axis=0, tiled=True)  72.9 us
    reduce_scatter x1, waiting for transfers between devices, body(): lax.psum_scatter(grad_triple, 'fsdp', scatter_dimension=0, tiled=True)  69.1 us
    pallas_call x1, Pallas kernels, attend_back(): pl.pallas_call(functools.partial(back_kernel, plan), name='attend_back',...  66.9 us
    all_gather x1, waiting for transfers between devices, body(): lax.all_gather(down_weight, 'fsdp', axis=0, tiled=True)  64.3 us
    reduce_scatter x1, waiting for transfers between devices, body(): lax.psum_scatter(dk.reshape(plan.keys, width), 'ctx', scatter_dimension=0...  53.6 us
    reduce_scatter x1, waiting for transfers between devices, body(): lax.psum_scatter(dv.reshape(plan.keys, width), 'ctx', scatter_dimension=0...  52.1 us
  transfers between devices with their start and end apart: 15, of which 13 were waited for; matrix products, arithmetic and copies ran while one was open for 7% of the time, Pallas kernels for 5%

profile of v1, /device:TPU:0, one launch (start us, length us, event | category | flops | bytes accessed | tf_op | source)
XLA Modules:
  0.0 979.8 jit_solution(15273286665039757573)
XLA Ops:
  14.0 13.9 %all-reduce.8 = (bf16[768]{0:T(1024)(128)(2,1)S(1)}, bf16[768]{0:T(1024)(128)(2,1)S(1)}, bf16[768]{0:T(1024)(128)(2,1)S(1)}, bf16[768]{0:T(1024)(128)(2,1)S(1)}) all-reduce(bf16[768]{0:T(1024)(128)(2,1)S(1)} %dynamic-update-slice.3, bf16[768]{0:T(1024)(128)(2,1)S(1)} %dynamic-update-slice.2, ...), channel_id=1, replica_groups=mesh['ctx'=8,'fsdp'=4] {'fsdp'}, use_global_device_ids=true, to_apply=%add.4 | all-reduce | flops 3072 | bytes 12288
  30.5 52.0 %all-gather.7.cloned.1.call-done = bf16[768,2304]{1,0:T(8,128)(2,1)} async-done(((bf16[192,2304]{1,0:T(8,128)(2,1)}), bf16[768,2304]{1,0:T(8,128)(2,1)}) %all-gather.7.cloned.1.call-update) | async-done | bytes 3538960 | tf_op jit(solution)/shard_map/all_gather | solution.py:598
  95.4 8.2 all-to-all-done
  107.9 64.3 %all-gather.15.cloned.1.call-done = bf16[3072,768]{1,0:T(8,128)(2,1)} async-done(((bf16[768,768]{1,0:T(8,128)(2,1)}), bf16[3072,768]{1,0:T(8,128)(2,1)}) %all-gather.15.cloned.1.call-update) | async-done | bytes 4718608 | tf_op jit(solution)/shard_map/all_gather | solution.py:603
  172.2 6.0 fusion.50
  178.2 49.9 %all-gather.9.cloned.1.call-done.kv.k_ref = bf16[2560,1664]{1,0:T(8,128)(2,1)} async-done(((bf16[320,1664]{1,0:T(8,128)(2,1)}), bf16[2560,1664]{1,0:T(8,128)(2,1)}) %all-gather.9.cloned.1.call-update) | async-done | bytes 8519696 | tf_op jit(solution)/shard_map/all_gather | solution.py:621
  228.1 46.6 %attend.1 = (bf16[8,40,768]{2,1,0:T(8,128)(2,1)}, bf16[8,40,768]{2,1,0:T(8,128)(2,1)}, f32[1,2,8,256]{3,2,1,0:T(8,128)}) custom-call(s32[11]{0:T(128)} %pad_add_fusion.meta, bf16[8,40,768]{2,1,0:T(8,128)(2,1)} %bitcast.75, bf16[2560,1664]{1,0:T(8,128)(2,1)} %all-gather.9.cloned.1.call-done.kv.k_ref), custom_call_target="tpu_custom_call" | custom-call | flops 2516582400 | bytes 7864320 | tf_op jit(solution)/shard_map/attend/pallas_call | solution.py:224
  277.0 72.9 %all-gather.13.cloned.1.call-done = bf16[768,3072]{1,0:T(8,128)(2,1)} async-done(((bf16[192,3072]{1,0:T(8,128)(2,1)}), bf16[768,3072]{1,0:T(8,128)(2,1)}) %all-gather.13.cloned.1.call-update) | async-done | bytes 4718608 | tf_op jit(solution)/shard_map/all_gather | solution.py:602
  349.9 8.7 fusion.6
  363.5 66.9 %attend_back.1 = (f32[8,40,768]{2,1,0:T(8,128)}, bf16[8,320,768]{2,1,0:T(8,128)(2,1)}, bf16[8,320,768]{2,1,0:T(8,128)(2,1)}, f32[36,320,128]{2,1,0:T(8,128)}, f32[8,320,128]{2,1,0:T(8,128)}) custom-call(s32[11]{0:T(128)} %pad_add_fusion.meta, bf16[8,40,768]{2,1,0:T(8,128)(2,1)} %bitcast.76, f32[8,40,768]{2,1,0:T(8,128)} %bitcast.74, ...), custom_call_target="tpu_custom_call" | custom-call | flops 6291456000 | bytes 23592960 | tf_op jit(solution)/shard_map/attend_back/pallas_call | solution.py:411
  434.8 11.1 %all-gather = f32[64,2560]{1,0:T(8,128)} all-gather(f32[8,2560]{1,0:T(8,128)S(1)} %bitcast.78), channel_id=2, replica_groups=mesh['ctx'=8,'fsdp'=4] {'ctx'}, dimensions={0}, use_global_device_ids=true | all-gather | bytes 737280 | tf_op jit(solution)/shard_map/all_gather | solution.py:647
  451.5 13.1 %first_head.1 = (f32[8,40,128]{2,1,0:T(8,128)}, f32[8,320,128]{2,1,0:T(8,128)}) custom-call(s32[11]{0:T(128)} %pad_add_fusion.meta, bf16[8,40,768]{2,1,0:T(8,128)(2,1)} %bitcast.77, bf16[2560,1664]{1,0:T(8,128)(2,1)} %all-gather.9.cloned.1.call-done.kv.k_ref, f32[8,320,128]{2,1,0:T(8,128)} %fusion.31.later_ref, f32[36,320,128]{2,1,0:T(8,128)} %get-tuple-element.27.within_ref), custom_call_target="tpu_custom_call" | custom-call | flops 314572800 | bytes 2621440 | tf_op jit(solution)/shard_map/first_head/pallas_call | solution.py:529
  468.1 7.3 convolution_convert_fusion
  475.5 6.1 convolution_convert_fusion.1
  488.2 14.5 %reduce-scatter.10.cloned.1.call-done = f32[320,128]{1,0:T(8,128)} async-done(((f32[2560,128]{1,0:T(8,128)}), f32[320,128]{1,0:T(8,128)}) %reduce-scatter.10.cloned.1.call-update) | async-done | bytes 163856 | tf_op jit(solution)/shard_map/reduce_scatter | solution.py:666
  502.7 53.6 %reduce-scatter.8.cloned.1.call-done = bf16[320,768]{1,0:T(8,128)(2,1)} async-done(((bf16[2560,768]{1,0:T(8,128)(2,1)}), bf16[320,768]{1,0:T(8,128)(2,1)}) %reduce-scatter.8.cloned.1.call-update) | async-done | bytes 491536 | tf_op jit(solution)/shard_map/reduce_scatter | solution.py:660
  558.2 52.1 %reduce-scatter.12.cloned.1.call-done = bf16[320,768]{1,0:T(8,128)(2,1)} async-done(((bf16[2560,768]{1,0:T(8,128)(2,1)}), bf16[320,768]{1,0:T(8,128)(2,1)}) %reduce-scatter.12.cloned.1.call-update) | async-done | bytes 491536 | tf_op jit(solution)/shard_map/reduce_scatter | solution.py:663
  617.5 7.2 fusion.10
  627.0 14.9 %reduce-scatter.16.cloned.1.call-done = bf16[192,768]{1,0:T(8,128)(2,1)} async-done(((bf16[768,768]{1,0:T(8,128)(2,1)}), bf16[192,768]{1,0:T(8,128)(2,1)}) %reduce-scatter.16.cloned.1.call-update) | async-done | bytes 294928 | tf_op jit(solution)/shard_map/reduce_scatter | solution.py:692
  641.8 86.1 %reduce-scatter.20.cloned.1.call-done = bf16[768,768]{1,0:T(8,128)(2,1)} async-done(((bf16[3072,768]{1,0:T(8,128)(2,1)}), bf16[768,768]{1,0:T(8,128)(2,1)}) %reduce-scatter.20.cloned.1.call-update) | async-done | bytes 1179664 | tf_op jit(solution)/shard_map/reduce_scatter | solution.py:694
  728.0 88.1 %reduce-scatter.18.cloned.1.call-done = bf16[192,3072]{1,0:T(8,128)(2,1)} async-done(((bf16[768,3072]{1,0:T(8,128)(2,1)}), bf16[192,3072]{1,0:T(8,128)(2,1)}) %reduce-scatter.18.cloned.1.call-update) | async-done | bytes 1179664 | tf_op jit(solution)/shard_map/reduce_scatter | solution.py:693
  816.1 69.1 %reduce-scatter.14.cloned.1.call-done = bf16[192,2304]{1,0:T(8,128)(2,1)} async-done(((bf16[768,2304]{1,0:T(8,128)(2,1)}), bf16[192,2304]{1,0:T(8,128)(2,1)}) %reduce-scatter.14.cloned.1.call-update) | async-done | bytes 884752 | tf_op jit(solution)/shard_map/reduce_scatter | solution.py:691
  890.1 44.0 %psum.35 = f32[4,768]{1,0:T(4,128)S(1)} all-reduce(f32[4,768]{1,0:T(4,128)S(1)} %pad_maximum_fusion.5), channel_id=1, replica_groups=mesh['ctx'=8,'fsdp'=4] {'ctx','fsdp'}, use_global_device_ids=true, to_apply=%region_22.25 | all-reduce | flops 3072 | bytes 24576 | tf_op jit(solution)/shard_map/psum | solution.py:699
  938.0 27.5 %all-reduce.11.cloned.1.call-done = (bf16[192,2304]{1,0:T(8,128)(2,1)}, bf16[192,768]{1,0:T(8,128)(2,1)}, bf16[192,3072]{1,0:T(8,128)(2,1)}, bf16[768,768]{1,0:T(8,128)(2,1)}) async-done(((bf16[192,2304]{1,0:T(8,128)(2,1)}, bf16[192,768]{1,0:T(8,128)(2,1)}, bf16[192,3072]{1,0:T(8,128)(2,1)}, bf16[768,768]{1,0:T(8,128)(2,1)}), (bf16[192,2304]{1,0:T(8,128)(2,1)}, bf16[192,768]{1,0:T(8,128)(2,1)}, ...) | async-done | bytes 3538960 | tf_op jit(solution)/shard_map/psum | solution.py:696
  (148 shorter events, 80.7 us)
Async XLA Ops:
  7.2 76.7 %copy-start = (bf16[320,768]{1,0:T(8,128)(2,1)S(1)}, bf16[320,768]{1,0:T(8,128)(2,1)}, u32[]{:S(2)}) copy-start(bf16[320,768]{1,0:T(8,128)(2,1)} %param.16) | copy-start | bytes 1474564
  7.2 75.3 %all-gather.7.cloned.1.call-start = ((), (), s32[]{:S(2)}) async-start(), calls=%async_computation.9 | async-start | bytes 4423680 | tf_op jit(solution)/shard_map/all_gather | solution.py:598
  7.9 164.2 %all-gather.15.cloned.1.call-start = ((), (), s32[]{:S(2)}) async-start(), calls=%async_computation.13 | async-start | bytes 5898240 | tf_op jit(solution)/shard_map/all_gather | solution.py:603
  8.7 219.4 %all-gather.9.cloned.1.call-start = ((), (), s32[]{:S(2)}) async-start(), calls=%async_computation.10 | async-start | bytes 9584640 | tf_op jit(solution)/shard_map/all_gather | solution.py:621
  86.6 8.1 copy-start.15
  87.7 187.0 %all-gather.11.cloned.1.call-start = ((), (), s32[]{:S(2)}) async-start(), calls=%async_computation.11 | async-start | bytes 1474560 | tf_op jit(solution)/shard_map/all_gather | solution.py:599
  88.3 261.7 %all-gather.13.cloned.1.call-start = ((), (), s32[]{:S(2)}) async-start(), calls=%async_computation.12 | async-start | bytes 5898240 | tf_op jit(solution)/shard_map/all_gather | solution.py:602
  89.0 83.1 %copy-start.8 = (bf16[320,768]{1,0:T(8,128)(2,1)S(1)}, bf16[320,768]{1,0:T(8,128)(2,1)}, u32[]{:S(2)}) copy-start(bf16[320,768]{1,0:T(8,128)(2,1)} %param.27) | copy-start | bytes 1474564
  90.5 13.1 %all-to-all-start = ((bf16[8,40,768]{2,1,0:T(8,128)(2,1)}), bf16[8,40,768]{2,1,0:T(8,128)(2,1)S(1)}, u32[]{:S(2)}, u32[]{:S(2)}) async-start(bf16[8,40,768]{2,1,0:T(8,128)(2,1)} %broadcast_select_fusion.1), calls=%async_computation | async-start | bytes 983040 | tf_op jit(solution)/shard_map/all_to_all | solution.py:611
  94.2 408.5 %reduce-scatter.10.cloned.1.call-start = ((), (), s32[]{:S(2)}) async-start(), calls=%async_computation.15 | async-start | bytes 1474560 | tf_op jit(solution)/shard_map/reduce_scatter | solution.py:666
  349.9 8.7 copy-start.13
  464.6 91.7 %reduce-scatter.8.cloned.1.call-start = ((), (), s32[]{:S(2)}) async-start(), calls=%async_computation.14 | async-start | bytes 4423680 | tf_op jit(solution)/shard_map/reduce_scatter | solution.py:660
  465.4 144.9 %reduce-scatter.12.cloned.1.call-start = ((), (), s32[]{:S(2)}) async-start(), calls=%async_computation.16 | async-start | bytes 4423680 | tf_op jit(solution)/shard_map/reduce_scatter | solution.py:663
  466.1 175.7 %reduce-scatter.16.cloned.1.call-start = ((), (), s32[]{:S(2)}) async-start(), calls=%async_computation.18 | async-start | bytes 1474560 | tf_op jit(solution)/shard_map/reduce_scatter | solution.py:692
  468.1 259.9 %reduce-scatter.20.cloned.1.call-start = ((), (), s32[]{:S(2)}) async-start(), calls=%async_computation.20 | async-start | bytes 5898240 | tf_op jit(solution)/shard_map/reduce_scatter | solution.py:694
  475.4 340.6 %reduce-scatter.18.cloned.1.call-start = ((), (), s32[]{:S(2)}) async-start(), calls=%async_computation.19 | async-start | bytes 5898240 | tf_op jit(solution)/shard_map/reduce_scatter | solution.py:693
  481.7 403.5 %reduce-scatter.14.cloned.1.call-start = ((), (), s32[]{:S(2)}) async-start(), calls=%async_computation.17 | async-start | bytes 4423680 | tf_op jit(solution)/shard_map/reduce_scatter | solution.py:691
  615.2 350.3 %all-reduce.11.cloned.1.call-start = ((), (), s32[]{:S(2)}) async-start(), calls=%async_computation.21 | async-start | bytes 7077888 | tf_op jit(solution)/shard_map/psum | solution.py:696
  617.4 7.3 copy-start.3
  617.4 7.2 copy-start.10
  617.4 7.2 copy-start.11
  617.4 7.2 copy-start.14
  627.0 258.3 %copy-start.4 = (f32[320,768]{1,0:T(8,128)S(1)}, f32[320,768]{1,0:T(8,128)}, u32[]{:S(2)}) copy-start(f32[320,768]{1,0:T(8,128)} %copy-done.3) | copy-start | bytes 2949124
  886.4 48.4 %all-to-all-start.1 = ((bf16[8,40,768]{2,1,0:T(8,128)(2,1)}), bf16[8,40,768]{2,1,0:T(8,128)(2,1)S(1)}, u32[]{:S(2)}, u32[]{:S(2)}) async-start(bf16[8,40,768]{2,1,0:T(8,128)(2,1)} %bitcast.17), calls=%async_computation.1 | async-start | bytes 983040 | tf_op jit(solution)/shard_map/all_to_all | solution.py:679
  (8 other events, 21.3 us)
Sparse Core Ops, SparseCore 0:
  9.6 72.8 all-gather.6
  84.0 88.1 all-gather.14
  174.6 53.3 all-gather.8
  229.5 30.4 all-gather.10
  261.4 88.5 all-gather.12
  464.7 37.9 reduce-scatter.9
  506.2 50.0 reduce-scatter.7
  560.2 50.0 reduce-scatter.11
  612.6 29.1 reduce-scatter.15
  644.0 83.9 reduce-scatter.19
  730.3 85.7 reduce-scatter.17
  818.3 66.8 reduce-scatter.13
  888.9 76.6 all-reduce.10
